TPU v7x, 32 devices: a whole 2x2x4 slice. The times are simulated.
32 devices in a mesh: wide: 16 (over z, y, x), narrow: 2 (over core).
Axes of the slice: x: 2, y: 2, z: 4, core: 2. Of those that a mesh axis runs over, the one named last changes fastest.
Arguments:
- grads: bfloat16 [14, 512, 2048], P(None, 'wide', 'narrow'), may hold values from -200 to 200
- momentum: float32 [14, 512, 2048], P(None, 'wide', 'narrow'), may hold values from -400 to 400
- owners: int32 [14], replicated, may hold values from 0 to 15, as said below
- norm_grads: float32 [28, 2048], P('narrow', 'wide'), may hold values from -6 to 6
- norm_params: float32 [28, 2048], P('narrow', 'wide'), may hold values from 0.5 to 1.5
- adam_m: float32 [28, 2048], P('narrow', 'wide'), may hold values from -4 to 4
- adam_v: float32 [28, 2048], P('narrow', 'wide'), may hold values from 0.1 to 4
Outputs:
- muon_update: bfloat16 [14, 512, 2048], P(None, 'wide', 'narrow')
- momentum_new: float32 [14, 512, 2048], P(None, 'wide', 'narrow')
- owner_load: float32 [16], P('wide')
- norm_params_new: float32 [28, 2048], P('narrow', 'wide')
- adam_m_new: float32 [28, 2048], P('narrow', 'wide')
- adam_v_new: float32 [28, 2048], P('narrow', 'wide')
Inputs may be any that keep to these rules, and one draw needn't show every extreme that they name: `owners`: each of the 16 groups owns at most 2 matrices, and some group owns exactly 2.
All inputs are finite; a program needn't handle non-finite values.
Results may differ from a plain program's by a relative error of at most 0.014.
Values may be sent and summed in bfloat16 or wider, within the bound.
A program may use at most 64 MiB of HBM per device.

v0:
```python
import math
import jax
import jax.numpy as jnp
from jax import lax
from jax.sharding import PartitionSpec as P

D = 2048
KV_OUT = 512
ITERS = 2
coef_a = 3.4445
coef_b = -4.775
coef_c = 2.0315
muon_beta = 0.95
norm_eps = 1e-07
adam_first = 0.9
adam_second = 0.95
adam_rate = 0.02
adam_eps = 1e-08
first_fix = 1.0 - 0.9**10
second_fix = 1.0 - 0.95**10


def polynomial_times(current, partial_value):
    gram_sum = lax.psum(partial_value.astype(jnp.bfloat16), "narrow")
    square = jnp.einsum("cmk,ckn->cmn", gram_sum, gram_sum, preferred_element_type=jnp.float32)
    polynomial = (coef_b * gram_sum.astype(jnp.float32) + coef_c * square).astype(jnp.bfloat16)
    return jnp.einsum("cmk,ckn->cmn", polynomial, current, preferred_element_type=jnp.float32)


def newton_schulz(current):
    result = current.astype(jnp.float32)
    for iteration in range(ITERS):
        partial_value = jnp.einsum(
            "cmk,cnk->cmn", current, current, preferred_element_type=jnp.float32
        )
        product_bx = polynomial_times(current, partial_value)
        result = coef_a * current.astype(jnp.float32) + product_bx
        if iteration + 1 < ITERS:
            current = result.astype(jnp.bfloat16)
    updates = (math.sqrt(D) * result).astype(jnp.bfloat16)
    update_values = updates.astype(jnp.float32)
    update_squares = lax.psum(jnp.sum(update_values * update_values, axis=(1, 2)), "narrow")
    return (updates[None], (update_squares / (KV_OUT * D))[None])


def orthogonalize(slot_block):
    directions = slot_block[0]
    square_sums = lax.psum(jnp.sum(directions * directions, axis=(1, 2)), "narrow")
    current = (directions / (jnp.sqrt(square_sums)[:, None, None] + norm_eps)).astype(jnp.bfloat16)
    return newton_schulz(current)


def on_device(grads, momentum, owners, norm_grads, norm_params, adam_m, adam_v):
    grad_values = grads.astype(jnp.float32)
    momentum_new = muon_beta * momentum + grad_values
    direction = grad_values + muon_beta * momentum_new
    groups = lax.axis_size("wide")
    matrix_count = owners.shape[0]
    matrix_ids = jnp.arange(matrix_count, dtype=jnp.int32)
    capacity = -(-matrix_count // groups)
    slot_of = matrix_ids % groups * capacity + matrix_ids // groups
    slot_total = groups * capacity
    slot_match = slot_of[None, :] == jnp.arange(slot_total, dtype=jnp.int32)[:, None]
    source = jnp.sum(jnp.where(slot_match, matrix_ids[None, :], 0), axis=1) + jnp.where(
        jnp.any(slot_match, axis=1), 0, matrix_count
    )
    row_count = direction.shape[1]
    col_count = direction.shape[2]
    padded = jnp.concatenate([direction, jnp.zeros((1, row_count, col_count), jnp.float32)], axis=0)
    outgoing = jnp.take(padded, source, axis=0).reshape(groups, capacity, row_count, col_count)
    updates, slot_loads = orthogonalize(
        lax.all_to_all(outgoing, "wide", split_axis=0, concat_axis=2, tiled=True)
    )
    returned = lax.all_to_all(updates, "wide", split_axis=2, concat_axis=0, tiled=True)
    arrived = returned.reshape(slot_total, row_count, col_count)
    muon_update = jnp.take(arrived, slot_of, axis=0)
    own_group = lax.axis_index("wide")
    computed_here = matrix_ids % groups == own_group
    local_loads = jnp.where(computed_here, jnp.take(slot_loads[0], matrix_ids // groups), 0.0)
    matrix_loads = lax.psum(local_loads, "wide")
    owner_load = jnp.sum(jnp.where(owners == own_group, matrix_loads, 0.0)).reshape(1)
    adam_m_new = adam_first * adam_m + (1.0 - adam_first) * norm_grads
    adam_v_new = adam_second * adam_v + (1.0 - adam_second) * norm_grads * norm_grads
    corrected = adam_m_new / first_fix / (jnp.sqrt(adam_v_new / second_fix) + adam_eps)
    norm_params_new = norm_params - adam_rate * corrected
    return (muon_update, momentum_new, owner_load, norm_params_new, adam_m_new, adam_v_new)


def solution(mesh):
    return jax.shard_map(
        on_device,
        mesh=mesh,
        in_specs=(
            P(None, "wide", "narrow"),
            P(None, "wide", "narrow"),
            P(),
            P("narrow", "wide"),
            P("narrow", "wide"),
            P("narrow", "wide"),
            P("narrow", "wide"),
        ),
        out_specs=(
            P(None, "wide", "narrow"),
            P(None, "wide", "narrow"),
            P("wide"),
            P("narrow", "wide"),
            P("narrow", "wide"),
            P("narrow", "wide"),
        ),
        check_vma=False,
    )
```

profile of v0, /device:TPU:0, one launch (start us, length us, event | category | flops | bytes accessed | tf_op | source)
XLA Modules:
  0.0 207.1 jit_solution(12475647661025235217)
XLA Ops:
  7.2 0.0 all-reduce.4.cloned.1.call-start
  7.2 0.1 fusion.20
  7.3 0.1 select_reduce_fusion
  7.5 3.5 %convert_add_fusion = (f32[14,32,1024]{2,1,0:T(8,128)S(1)}, f32[14,32,1024]{2,1,0:T(8,128)}) fusion(bf16[14,32,1024]{2,1,0:T(8,128)(2,1)} %param.7, f32[14,32,1024]{2,1,0:T(8,128)} %param.8), kind=kLoop, calls=%fused_computation.2 | loop fusion | flops 2293760 | bytes 6422528 | tf_op jit(solution)/shard_map/add | solution.py:56
  11.0 0.3 concatenate.3
  11.2 2.0 gather_fusion
  13.3 1.8 bitcast_select_fusion
  15.1 57.0 %all_to_all.8 = f32[16,1,32,1024]{3,2,1,0:T(8,128)S(1)} all-to-all(f32[16,1,32,1024]{3,2,1,0:T(8,128)S(1)} %bitcast_select_fusion), channel_id=1, replica_groups=mesh['wide'=16,'narrow'=2] {'wide'}, dimensions={0} | all-to-all | bytes 4194304 | tf_op jit(solution)/shard_map/all_to_all | solution.py:72
  72.1 1.1 multiply_reduce_fusion.1
  73.2 3.1 %psum.35 = f32[1]{0:T(128)} all-reduce(f32[1]{0:T(128)} %bitcast.3), channel_id=1, replica_groups=mesh['wide'=16,'narrow'=2] {'narrow'}, use_global_device_ids=true, to_apply=%region_3.4 | all-reduce | flops 1 | bytes 8 | tf_op jit(solution)/shard_map/psum | solution.py:48
  77.0 1.7 convert_multiply_fusion
  78.7 0.0 copy-start
  78.7 1.5 fusion.7
  80.2 0.0 all-reduce.4.cloned.1.call-update
  80.3 0.2 all-reduce.6.cloned.1.call-start
  80.5 16.9 %all-reduce.4.cloned.1.call-done = bf16[1,512,512]{2,1,0:T(8,128)(2,1)} async-done(((bf16[1,512,512]{2,1,0:T(8,128)(2,1)}), bf16[1,512,512]{2,1,0:T(8,128)(2,1)}) %all-reduce.4.cloned.1.call-update) | async-done | bytes 524304 | tf_op jit(solution)/shard_map/psum | solution.py:24
  97.4 0.0 copy-done
  97.4 3.4 %fusion = bf16[512,1024]{1,0:T(8,128)(2,1)} fusion(f32[16,1,32,1024]{3,2,1,0:T(8,128)S(1)} %copy-done, bf16[512,1024]{1,0:T(8,128)(2,1)S(1)} %bitcast.81, bf16[1,512,512]{2,1,0:T(8,128)(2,1)} %all-reduce.4.cloned.1.call-done), kind=kOutput, calls=%fused_computation.5 | convolution fusion | flops 807665664 | bytes 4718592 | tf_op jit(solution)/shard_map/cmk,ckn->cmn/dot_general | solution.py:27
  100.8 0.0 copy-start.6
  100.8 3.2 %fusion.8 = bf16[1,512,512]{2,1,0:T(8,128)(2,1)} fusion(bf16[512,1024]{1,0:T(8,128)(2,1)} %fusion), kind=kOutput, calls=%fused_computation.23 | convolution fusion | flops 537133056 | bytes 1572864 | tf_op jit(solution)/shard_map/cmk,cnk->cmn/dot_general | solution.py:33
  104.0 0.0 all-reduce.6.cloned.1.call-update
  104.0 20.1 %all-reduce.6.cloned.1.call-done = bf16[1,512,512]{2,1,0:T(8,128)(2,1)} async-done(((bf16[1,512,512]{2,1,0:T(8,128)(2,1)}), bf16[1,512,512]{2,1,0:T(8,128)(2,1)}) %all-reduce.6.cloned.1.call-update) | async-done | bytes 524304 | tf_op jit(solution)/shard_map/psum | solution.py:24
  124.1 0.0 copy-done.6
  124.1 3.2 %multiply_reduce_fusion = (f32[]{:T(128)}, bf16[512,1024]{1,0:T(8,128)(2,1)S(1)}) fusion(bf16[512,1024]{1,0:T(8,128)(2,1)S(1)} %copy-done.6, bf16[1,512,512]{2,1,0:T(8,128)(2,1)} %all-reduce.6.cloned.1.call-done), kind=kOutput, calls=%fused_computation.7 | convolution fusion | flops 810811392 | bytes 2621444 | tf_op jit(solution)/shard_map/cmk,ckn->cmn/dot_general | solution.py:27
  127.3 1.6 copy.18
  128.9 0.5 broadcast.355
  129.5 6.8 %reduce.3 = bf16[512,1024]{1,0:T(8,128)(2,1)S(1)} reduce(bf16[512,1,1,1024]{3,2,1,0:T(2,128)(2,1)S(1)} %bitcast.77, bf16[]{:T(256)} %broadcast.355), dimensions={1,2}, to_apply=%bitcast.75.reduce_sub_computation | reduce | bytes 2097154
  136.2 0.0 copy-start.1
  136.3 0.0 copy-start.2
  136.3 0.0 copy-start.3
  136.3 0.0 copy-start.4
  136.3 0.0 copy-start.5
  136.3 1.6 reshape.253
  137.9 6.8 %all-to-all-start.1 = ((bf16[16,2,16384]{2,1,0:T(2,128)(2,1)}), bf16[16,2,16384]{2,1,0:T(2,128)(2,1)S(1)}, u32[]{:S(2)}, u32[]{:S(2)}) async-start(bf16[16,2,16384]{2,1,0:T(2,128)(2,1)} %reshape.253), calls=%async_computation.1 | async-start | bytes 2097152 | tf_op jit(solution)/shard_map/all_to_all | solution.py:74
  144.7 0.0 copy-done.1
  144.8 0.0 copy-done.2
  144.8 0.0 copy-done.3
  144.8 0.0 copy-done.4
  144.8 0.6 multiply_subtract_fusion
  145.4 3.1 %psum.38 = f32[1]{0:T(128)} all-reduce(f32[1]{0:T(128)} %bitcast.17), channel_id=1, replica_groups=mesh['wide'=16,'narrow'=2] {'narrow'}, use_global_device_ids=true, to_apply=%region_7.8 | all-reduce | flops 1 | bytes 8 | tf_op jit(solution)/shard_map/psum | solution.py:42
  149.2 47.4 %psum.39 = f32[14]{0:T(128)S(1)} all-reduce(f32[14]{0:T(128)S(1)} %compare_select_fusion.5), channel_id=1, replica_groups=mesh['wide'=16,'narrow'=2] {'wide'}, use_global_device_ids=true, to_apply=%region_8.9 | all-reduce | flops 14 | bytes 112 | tf_op jit(solution)/shard_map/psum | solution.py:80
  196.6 0.0 copy-done.5
  196.6 0.6 fusion.23
  197.2 0.0 all-to-all-done.1
  197.2 1.0 reshape.254
  198.2 0.4 copy.16
  198.6 0.6 gather_fusion.1
  199.2 1.1 broadcast_select_fusion
  (8 shorter events, 0.1 us)
Async XLA Ops:
  7.2 90.2 %all-reduce.4.cloned.1.call-start = ((), (), s32[]{:S(2)}) async-start(), calls=%async_computation.2 | async-start | bytes 1048576 | tf_op jit(solution)/shard_map/psum | solution.py:24
  78.7 18.7 %copy-start = (f32[16,1,32,1024]{3,2,1,0:T(8,128)S(1)}, f32[16,1,32,1024]{3,2,1,0:T(8,128)}, u32[]{:S(2)}) copy-start(f32[16,1,32,1024]{3,2,1,0:T(8,128)} %get-tuple-element.9) | copy-start | bytes 6291460
  80.3 43.8 %all-reduce.6.cloned.1.call-start = ((), (), s32[]{:S(2)}) async-start(), calls=%async_computation.3 | async-start | bytes 1048576 | tf_op jit(solution)/shard_map/psum | solution.py:24
  100.8 23.3 %copy-start.6 = (bf16[512,1024]{1,0:T(8,128)(2,1)S(1)}, bf16[512,1024]{1,0:T(8,128)(2,1)}, u32[]{:S(2)}) copy-start(bf16[512,1024]{1,0:T(8,128)(2,1)} %fusion) | copy-start | bytes 3145732
  136.2 8.5 %copy-start.1 = (f32[14,128]{1,0:T(8,128)S(1)}, f32[14,128]{1,0:T(8,128)}, u32[]{:S(2)}) copy-start(f32[14,128]{1,0:T(8,128)} %param.11) | copy-start | bytes 21508
  136.3 8.5 %copy-start.2 = (f32[14,128]{1,0:T(8,128)S(1)}, f32[14,128]{1,0:T(8,128)}, u32[]{:S(2)}) copy-start(f32[14,128]{1,0:T(8,128)} %param.10) | copy-start | bytes 21508
  136.3 8.5 %copy-start.3 = (f32[14,128]{1,0:T(8,128)S(1)}, f32[14,128]{1,0:T(8,128)}, u32[]{:S(2)}) copy-start(f32[14,128]{1,0:T(8,128)} %param.12) | copy-start | bytes 21508
  136.3 8.5 %copy-start.4 = (f32[14,128]{1,0:T(8,128)S(1)}, f32[14,128]{1,0:T(8,128)}, u32[]{:S(2)}) copy-start(f32[14,128]{1,0:T(8,128)} %param.13) | copy-start | bytes 21508
  136.3 60.3 %copy-start.5 = (s32[14]{0:T(128)S(1)}, s32[14]{0:T(128)}, u32[]{:S(2)}) copy-start(s32[14]{0:T(128)} %param.9) | copy-start | bytes 172
  137.9 59.3 %all-to-all-start.1 = ((bf16[16,2,16384]{2,1,0:T(2,128)(2,1)}), bf16[16,2,16384]{2,1,0:T(2,128)(2,1)S(1)}, u32[]{:S(2)}, u32[]{:S(2)}) async-start(bf16[16,2,16384]{2,1,0:T(2,128)(2,1)} %reshape.253), calls=%async_computation.1 | async-start | bytes 2097152 | tf_op jit(solution)/shard_map/all_to_all | solution.py:74
Sparse Core Ops, SparseCore 0:
  80.4 16.9 all-reduce.3
  104.1 19.9 all-reduce.5
where the time goes:
time: 208 us; the launch traced here: 207 us
  blocking collectives  111 us (53%)
  waiting for transfers between devices  37 us (18%)
  other arithmetic  17.5 us (8%)
  between operations  15.6 us (8%)
  matrix products  11.3 us (5%)
  local copies, waits for them, and re-layouts  8.1 us (4%)
  starting transfers between devices  7.05 us (3%)
    all_to_all x1, blocking collectives, on_device(): lax.all_to_all(outgoing, 'wide', split_axis=0, concat_axis=2, tiled=True)  57 us
    psum x1, blocking collectives, on_device(): matrix_loads = lax.psum(local_loads, 'wide')  47.4 us
    psum x2, waiting for transfers between devices, polynomial_times(): gram_sum = lax.psum(partial_value.astype(jnp.bfloat16), 'narrow')  37 us
    all_to_all x1, starting transfers between devices, on_device(): lax.all_to_all(updates, 'wide', split_axis=2, concat_axis=0, tiled=True)  6.79 us
    unnamed x1, other arithmetic  6.78 us
    dot_general x2, matrix products, polynomial_times(): jnp.einsum('cmk,ckn->cmn', polynomial, current, preferred_element_type=jn...  6.64 us
    dot_general x2, matrix products, newton_schulz(): jnp.einsum('cmk,cnk->cmn', current, current, preferred_element_type=jnp.f...  4.71 us
  transfers between devices with their start and end apart: 3, of which 2 were waited for; matrix products, arithmetic and copies ran while one was open for 1% of the time, Pallas kernels for 0%

commit v1 on v0

--- a/solution.py
+++ b/solution.py
@@ -21,7 +21,7 @@
 
 
 def polynomial_times(current, partial_value):
-    gram_sum = lax.psum(partial_value.astype(jnp.bfloat16), "narrow")
+    gram_sum = jnp.sum(lax.all_gather(partial_value.astype(jnp.bfloat16), "narrow"), axis=0)
     square = jnp.einsum("cmk,ckn->cmn", gram_sum, gram_sum, preferred_element_type=jnp.float32)
     polynomial = (coef_b * gram_sum.astype(jnp.float32) + coef_c * square).astype(jnp.bfloat16)
     return jnp.einsum("cmk,ckn->cmn", polynomial, current, preferred_element_type=jnp.float32)

time: 208 us -> 191 us (0.918)
  waiting for transfers between devices: 37 us -> 17.6 us
  other arithmetic: 17.5 us -> 21.5 us
    psum x2 -> x0, waiting for transfers between devices: 37 us -> none  [polynomial_times(): gram_sum = lax.psum(partial_value.astype(jnp.bfloat16), 'narrow')]
    all_gather x0 -> x2, waiting for transfers between devices: none -> 17.6 us  [polynomial_times(): lax.all_gather(partial_value.astype(jnp.bfloat16), 'narrow')]
    reduce_sum x0 -> x2, other arithmetic: none -> 4.01 us  [polynomial_times(): jnp.sum(lax.all_gather(partial_value.astype(jnp.bfloat16), 'narrow'), axi...]
where the time goes in v1:
time: 191 us
  blocking collectives  111 us (58%)
  other arithmetic  21.5 us (11%)
  waiting for transfers between devices  17.6 us (9%)
  between operations  15.6 us (8%)
  matrix products  10.2 us (5%)
  local copies, waits for them, and re-layouts  8.1 us (4%)
  starting transfers between devices  7.03 us (4%)
    all_to_all x1, blocking collectives, on_device(): lax.all_to_all(outgoing, 'wide', split_axis=0, concat_axis=2, tiled=True)  57 us
    psum x1, blocking collectives, on_device(): matrix_loads = lax.psum(local_loads, 'wide')  47.4 us
    all_gather x2, waiting for transfers between devices, polynomial_times(): lax.all_gather(partial_value.astype(jnp.bfloat16), 'narrow')  17.6 us
    unnamed x1, other arithmetic  6.78 us
    all_to_all x1, starting transfers between devices, on_device(): lax.all_to_all(updates, 'wide', split_axis=2, concat_axis=0, tiled=True)  6.77 us
    dot_general x2, matrix products, polynomial_times(): jnp.einsum('cmk,ckn->cmn', polynomial, current, preferred_element_type=jn...  5.51 us
    dot_general x2, matrix products, newton_schulz(): jnp.einsum('cmk,cnk->cmn', current, current, preferred_element_type=jnp.f...  4.71 us
    reduce_sum x2, other arithmetic, polynomial_times(): jnp.sum(lax.all_gather(partial_value.astype(jnp.bfloat16), 'narrow'), axi...  4.01 us
  transfers between devices with their start and end apart: 3, of which 2 were waited for; matrix products, arithmetic and copies ran while one was open for 1% of the time, Pallas kernels for 0%

profile of v1, /device:TPU:0, one launch (start us, length us, event | category | flops | bytes accessed | tf_op | source)
XLA Modules:
  0.0 190.6 jit_solution(5172679001927111768)
XLA Ops:
  7.2 0.0 all-gather.5.cloned.1.call-start
  7.2 0.1 fusion.14
  7.3 0.1 select_reduce_fusion
  7.5 3.5 %convert_add_fusion = (f32[14,32,1024]{2,1,0:T(8,128)S(1)}, f32[14,32,1024]{2,1,0:T(8,128)}) fusion(bf16[14,32,1024]{2,1,0:T(8,128)(2,1)} %param.7, f32[14,32,1024]{2,1,0:T(8,128)} %param.8), kind=kLoop, calls=%fused_computation.2 | loop fusion | flops 2293760 | bytes 6422528 | tf_op jit(solution)/shard_map/add | solution.py:56
  11.0 0.3 concatenate.3
  11.2 2.0 %gather_fusion = f32[16,32,1024]{2,1,0:T(8,128)} fusion(f32[15,32,1024]{2,1,0:T(8,128)S(1)} %concatenate.3, s32[1024]{0:T(1024)S(1)} %pad_clamp_fusion.1), kind=kCustom, calls=%fused_computation | custom fusion | bytes 4194368 | tf_op jit(solution)/shard_map/jit(_take)/gather | solution.py:70
  13.3 1.8 bitcast_select_fusion
  15.1 57.0 %all_to_all.8 = f32[16,1,32,1024]{3,2,1,0:T(8,128)S(1)} all-to-all(f32[16,1,32,1024]{3,2,1,0:T(8,128)S(1)} %bitcast_select_fusion), channel_id=1, replica_groups=mesh['wide'=16,'narrow'=2] {'wide'}, dimensions={0} | all-to-all | bytes 4194304 | tf_op jit(solution)/shard_map/all_to_all | solution.py:72
  72.1 1.1 multiply_reduce_fusion.1
  73.2 3.1 %psum.21 = f32[1]{0:T(128)} all-reduce(f32[1]{0:T(128)} %bitcast.3), channel_id=1, replica_groups=mesh['wide'=16,'narrow'=2] {'narrow'}, use_global_device_ids=true, to_apply=%region_3.4 | all-reduce | flops 1 | bytes 8 | tf_op jit(solution)/shard_map/psum | solution.py:48
  77.0 1.7 convert_multiply_fusion
  78.7 0.0 copy-start
  78.7 1.5 convolution_convert_fusion.1
  80.2 0.0 all-gather.5.cloned.1.call-update
  80.3 0.2 all-gather.7.cloned.1.call-start
  80.5 7.2 %all-gather.5.cloned.1.call-done = bf16[1024,512]{1,0:T(8,128)(2,1)} async-done(((bf16[512,512]{1,0:T(8,128)(2,1)}), bf16[1024,512]{1,0:T(8,128)(2,1)}) %all-gather.5.cloned.1.call-update) | async-done | bytes 1048592 | tf_op jit(solution)/shard_map/all_gather | solution.py:24
  87.7 2.3 %reduce.7 = bf16[512,512]{1,0:T(8,128)(2,1)} reduce(bf16[2,512,512]{2,1,0:T(8,128)(2,1)} %bitcast.40, bf16[]{:T(256)} %constant.119.clone.1), dimensions={0}, to_apply=%region_4.5 | reduce | flops 262144 | bytes 1572866 | tf_op jit(solution)/shard_map/reduce_sum | solution.py:24
  90.1 0.0 copy-done
  90.1 3.6 %fusion = bf16[512,1024]{1,0:T(8,128)(2,1)} fusion(f32[16,1,32,1024]{3,2,1,0:T(8,128)S(1)} %copy-done, bf16[512,1024]{1,0:T(8,128)(2,1)S(1)} %bitcast.43, bf16[512,512]{1,0:T(8,128)(2,1)} %reduce.7), kind=kOutput, calls=%fused_computation.5 | convolution fusion | flops 807665664 | bytes 4718592 | tf_op jit(solution)/shard_map/cmk,ckn->cmn/dot_general | solution.py:27
  93.7 0.0 copy-start.6
  93.7 3.2 %convolution_convert_fusion = bf16[512,512]{1,0:T(8,128)(2,1)} fusion(bf16[512,1024]{1,0:T(8,128)(2,1)} %fusion), kind=kOutput, calls=%fused_computation.18 | convolution fusion | flops 537133056 | bytes 1572864 | tf_op jit(solution)/shard_map/cmk,cnk->cmn/dot_general | solution.py:33
  96.9 0.0 all-gather.7.cloned.1.call-update
  96.9 10.4 %all-gather.7.cloned.1.call-done = bf16[1024,512]{1,0:T(8,128)(2,1)} async-done(((bf16[512,512]{1,0:T(8,128)(2,1)}), bf16[1024,512]{1,0:T(8,128)(2,1)}) %all-gather.7.cloned.1.call-update) | async-done | bytes 1048592 | tf_op jit(solution)/shard_map/all_gather | solution.py:24
  107.3 1.7 reduce.8
  108.9 0.0 copy-done.6
  108.9 1.9 multiply_reduce_fusion
  110.8 1.6 copy.18
  112.4 0.5 broadcast.357
  112.9 6.8 %reduce.9 = bf16[512,1024]{1,0:T(8,128)(2,1)S(1)} reduce(bf16[512,1,1,1024]{3,2,1,0:T(2,128)(2,1)S(1)} %bitcast.37, bf16[]{:T(256)} %broadcast.357), dimensions={1,2}, to_apply=%bitcast.35.reduce_sub_computation | reduce | bytes 2097154
  119.7 0.0 copy-start.1
  119.7 0.0 copy-start.2
  119.8 0.0 copy-start.3
  119.8 0.0 copy-start.4
  119.8 0.0 copy-start.5
  119.8 1.6 reshape.267
  121.4 6.8 %all-to-all-start.1 = ((bf16[16,2,16384]{2,1,0:T(2,128)(2,1)}), bf16[16,2,16384]{2,1,0:T(2,128)(2,1)S(1)}, u32[]{:S(2)}, u32[]{:S(2)}) async-start(bf16[16,2,16384]{2,1,0:T(2,128)(2,1)} %reshape.267), calls=%async_computation.1 | async-start | bytes 2097152 | tf_op jit(solution)/shard_map/all_to_all | solution.py:74
  128.2 0.0 copy-done.1
  128.2 0.0 copy-done.2
  128.2 0.0 copy-done.3
  128.2 0.0 copy-done.4
  128.3 0.6 multiply_subtract_fusion
  128.9 3.1 %psum.22 = f32[1]{0:T(128)} all-reduce(f32[1]{0:T(128)} %bitcast.11), channel_id=1, replica_groups=mesh['wide'=16,'narrow'=2] {'narrow'}, use_global_device_ids=true, to_apply=%region_7.8 | all-reduce | flops 1 | bytes 8 | tf_op jit(solution)/shard_map/psum | solution.py:42
  132.6 47.4 %psum.23 = f32[14]{0:T(128)S(1)} all-reduce(f32[14]{0:T(128)S(1)} %compare_select_fusion.5), channel_id=1, replica_groups=mesh['wide'=16,'narrow'=2] {'wide'}, use_global_device_ids=true, to_apply=%region_8.9 | all-reduce | flops 14 | bytes 112 | tf_op jit(solution)/shard_map/psum | solution.py:80
  180.1 0.0 copy-done.5
  180.1 0.6 fusion.17
  180.7 0.0 all-to-all-done.1
  180.7 1.0 reshape.268
  181.7 0.4 copy.16
  182.1 0.6 gather_fusion.1
  182.7 1.1 broadcast_select_fusion
  (8 shorter events, 0.1 us)
Async XLA Ops:
  7.2 80.6 %all-gather.5.cloned.1.call-start = ((), (), s32[]{:S(2)}) async-start(), calls=%async_computation.2 | async-start | bytes 1572864 | tf_op jit(solution)/shard_map/all_gather | solution.py:24
  78.7 11.4 %copy-start = (f32[16,1,32,1024]{3,2,1,0:T(8,128)S(1)}, f32[16,1,32,1024]{3,2,1,0:T(8,128)}, u32[]{:S(2)}) copy-start(f32[16,1,32,1024]{3,2,1,0:T(8,128)} %get-tuple-element.9) | copy-start | bytes 6291460
  80.3 27.0 %all-gather.7.cloned.1.call-start = ((), (), s32[]{:S(2)}) async-start(), calls=%async_computation.3 | async-start | bytes 1572864 | tf_op jit(solution)/shard_map/all_gather | solution.py:24
  93.7 15.2 %copy-start.6 = (bf16[512,1024]{1,0:T(8,128)(2,1)S(1)}, bf16[512,1024]{1,0:T(8,128)(2,1)}, u32[]{:S(2)}) copy-start(bf16[512,1024]{1,0:T(8,128)(2,1)} %fusion) | copy-start | bytes 3145732
  119.7 8.5 %copy-start.1 = (f32[14,128]{1,0:T(8,128)S(1)}, f32[14,128]{1,0:T(8,128)}, u32[]{:S(2)}) copy-start(f32[14,128]{1,0:T(8,128)} %param.11) | copy-start | bytes 21508
  119.7 8.5 %copy-start.2 = (f32[14,128]{1,0:T(8,128)S(1)}, f32[14,128]{1,0:T(8,128)}, u32[]{:S(2)}) copy-start(f32[14,128]{1,0:T(8,128)} %param.10) | copy-start | bytes 21508
  119.8 8.5 %copy-start.3 = (f32[14,128]{1,0:T(8,128)S(1)}, f32[14,128]{1,0:T(8,128)}, u32[]{:S(2)}) copy-start(f32[14,128]{1,0:T(8,128)} %param.12) | copy-start | bytes 21508
  119.8 8.5 %copy-start.4 = (f32[14,128]{1,0:T(8,128)S(1)}, f32[14,128]{1,0:T(8,128)}, u32[]{:S(2)}) copy-start(f32[14,128]{1,0:T(8,128)} %param.13) | copy-start | bytes 21508
  119.8 60.3 %copy-start.5 = (s32[14]{0:T(128)S(1)}, s32[14]{0:T(128)}, u32[]{:S(2)}) copy-start(s32[14]{0:T(128)} %param.9) | copy-start | bytes 172
  121.4 59.3 %all-to-all-start.1 = ((bf16[16,2,16384]{2,1,0:T(2,128)(2,1)}), bf16[16,2,16384]{2,1,0:T(2,128)(2,1)S(1)}, u32[]{:S(2)}, u32[]{:S(2)}) async-start(bf16[16,2,16384]{2,1,0:T(2,128)(2,1)} %reshape.267), calls=%async_computation.1 | async-start | bytes 2097152 | tf_op jit(solution)/shard_map/all_to_all | solution.py:74
Sparse Core Ops, SparseCore 0:
  80.4 7.2 all-gather.4
  97.0 10.1 all-gather.6
